TPU v7x, 32 devices: a whole 2x2x4 slice. The times are simulated.
32 devices in a mesh: comp: 16 (over z, x, core), rows: 2 (over y).
Axes of the slice: x: 2, y: 2, z: 4, core: 2. Of those that a mesh axis runs over, the one named last changes fastest.
Arguments:
- hidden_states: bfloat16 [2, 2, 16, 128, 2560], P('rows', None, 'comp'), may hold values from -6 to 6
- queries: bfloat16 [2, 2, 16, 128, 1280], P('rows', None, 'comp'), may hold values from -900 to 900
- new_keys: bfloat16 [2, 2, 16, 128, 1280], P('rows', None, 'comp'), may hold values from -6 to 6
- new_values: bfloat16 [2, 2, 16, 128, 1280], P('rows', None, 'comp'), may hold values from -6 to 6
- out_grad: bfloat16 [2, 2, 16, 128, 1280], P('rows', None, 'comp'), may hold values from -6 to 6
- gate_weight: bfloat16 [2560, 128], replicated, may hold values from -0.125 to 0.125
- gate_bias: float32 [128], replicated, may hold values from -2 to 6
- prompt_state: float32 [2, 16, 2, 2, 2, 64, 640], P('rows', 'comp'), may hold values from -6 to 6
- owners: int32 [2, 2], P('rows'), may hold values from 0 to 15
- lengths: int32 [2, 2, 16], P('rows', None, 'comp'), may hold values from 32 to 128
- advantage: float32 [2, 2, 16], P('rows', None, 'comp'), may hold values from -4 to 4
Outputs:
- d_queries: bfloat16 [2, 2, 16, 128, 1280], P('rows', None, 'comp')
- d_keys: bfloat16 [2, 2, 16, 128, 1280], P('rows', None, 'comp')
- d_values: bfloat16 [2, 2, 16, 128, 1280], P('rows', None, 'comp')
- d_hidden: bfloat16 [2, 2, 16, 128, 2560], P('rows', None, 'comp')
- d_gate_weight: float32 [2560, 128], replicated
- d_gate_bias: float32 [128], replicated
- d_state: float32 [2, 2, 2, 2, 64, 640], P('rows', None, None, None, 'comp')
All inputs are finite; a program needn't handle non-finite values.
Results may differ from a plain program's by a relative error of at most 0.011.
Values sent between devices are 32-bit elements; how exact they have to be, the bound alone decides.
A program may use at most 64 MiB of HBM per device.

v0:
```python
import jax
import jax.numpy as jnp
from jax import lax
from jax.sharding import PartitionSpec as P


def broadcast(block, axis, holder):
    block = jnp.where(lax.axis_index(axis) == holder, block, jnp.zeros_like(block))
    return lax.psum(block, axis)


def slot_forward(gates, queries, keys_in, values_in, anchor_point):
    steps = queries.shape[0]
    heads = anchor_point.shape[1]
    slots = anchor_point.shape[2]
    width = anchor_point.shape[3]
    highest_score = lax.Precision.HIGHEST
    log_keep = jax.nn.log_sigmoid(gates).reshape(steps, heads, slots) / 8.0
    running = jnp.cumsum(log_keep, axis=0)
    inflow = -jnp.expm1(log_keep)
    places = jnp.arange(steps, dtype=jnp.int32)
    lower = (places[:, None] >= places[None, :])[:, :, None, None]
    between = running[:, None] - running[None, :]
    reach = jnp.where(lower, jnp.exp(jnp.where(lower, between, 0.0)), 0.0) * inflow[None]
    score_scale = width ** (-0.5)
    query_head_count = queries.astype(jnp.float32).reshape(steps, heads, width)
    key_heads = keys_in.astype(jnp.float32).reshape(steps, heads, width)
    value_heads = values_in.astype(jnp.float32).reshape(steps, heads, width)
    pairs = jnp.einsum("thd,jhd->thj", query_head_count, key_heads) * score_scale
    carried_state = jnp.exp(running)
    anchor_score_rows = (
        jnp.einsum("icv,crv->icr", query_head_count, anchor_point[0], precision=highest_score)
        * score_scale
    )
    scores = (
        jnp.einsum("tjhm,thj->thm", reach, pairs, precision=highest_score)
        + carried_state * anchor_score_rows
    )
    slot_probabilities = jax.nn.softmax(scores, axis=-1)
    mixing = jnp.einsum("thm,tjhm->thj", slot_probabilities, reach, precision=highest_score).astype(
        jnp.bfloat16
    )
    result_output = jnp.einsum("thj,jhd->thd", mixing.astype(jnp.float32), value_heads)
    result_output = result_output + jnp.einsum(
        "ivw,vwb->ivb", slot_probabilities * carried_state, anchor_point[1], precision=highest_score
    )
    return result_output.reshape(steps, heads * width)


def shards(
    hidden_states,
    queries,
    new_keys,
    new_values,
    out_grad,
    gate_weight,
    gate_bias,
    prompt_state,
    owners,
    lengths,
    advantage,
):
    local_states = prompt_state[0, 0]
    prompts = local_states.shape[0]
    steps = queries.shape[3]
    received = []
    for prompt in range(prompts):
        received.append(broadcast(local_states[prompt], "comp", owners[0, prompt]))
    anchors = jnp.stack(received)
    places = jnp.arange(steps, dtype=jnp.int32)
    sum_weight = jnp.zeros(gate_weight.shape, jnp.float32)
    sum_bias = jnp.zeros(gate_bias.shape, jnp.float32)
    state_terms = []
    out_q, out_k, out_v, out_x = ([], [], [], [])
    for prompt in range(prompts):
        list_q, list_k, list_v, list_x = ([], [], [], [])
        tokens = hidden_states[0, prompt, 0]
        gates = jnp.dot(tokens, gate_weight, preferred_element_type=jnp.float32) + gate_bias
        live = jnp.where(places < lengths[0, prompt, 0], 1.0, 0.0).astype(jnp.float32)
        cotangent = (advantage[0, prompt, 0] * live)[:, None] * out_grad[0, prompt, 0].astype(
            jnp.float32
        )
        result_output, pullback = jax.vjp(
            slot_forward,
            gates,
            queries[0, prompt, 0],
            new_keys[0, prompt, 0],
            new_values[0, prompt, 0],
            anchors[prompt],
        )
        grad_gates, grad_q, grad_k, grad_v, grad_anchor = pullback(cotangent)
        gates_low = grad_gates.astype(jnp.bfloat16)
        list_x.append(
            jnp.dot(gates_low, gate_weight.T, preferred_element_type=jnp.float32).astype(
                jnp.bfloat16
            )
        )
        sum_weight = sum_weight + jnp.dot(tokens.T, gates_low, preferred_element_type=jnp.float32)
        sum_bias = sum_bias + jnp.sum(grad_gates, axis=0)
        list_q.append(grad_q)
        list_k.append(grad_k)
        list_v.append(grad_v)
        state_terms.append(grad_anchor)
        out_q.append(jnp.stack(list_q))
        out_k.append(jnp.stack(list_k))
        out_v.append(jnp.stack(list_v))
        out_x.append(jnp.stack(list_x))
    state_grads = jnp.stack(state_terms)
    d_state, weight_block, bias_block = (
        lax.psum_scatter(state_grads, "comp", scatter_dimension=3, tiled=True),
        lax.psum_scatter(sum_weight, "comp", scatter_dimension=0, tiled=True),
        lax.psum_scatter(sum_bias, "comp", scatter_dimension=0, tiled=True),
    )
    weight_block, bias_block = lax.psum((weight_block, bias_block), "rows")
    d_weight, d_bias = (
        lax.all_gather(weight_block, "comp", axis=0, tiled=True),
        lax.all_gather(bias_block, "comp", axis=0, tiled=True),
    )
    return (
        jnp.stack(out_q)[None],
        jnp.stack(out_k)[None],
        jnp.stack(out_v)[None],
        jnp.stack(out_x)[None],
        d_weight,
        d_bias,
        d_state[None],
    )


def solution(mesh):
    placed = (
        P("rows", None, "comp", None, None),
        P("rows", None, "comp", None, None),
        P("rows", None, "comp", None, None),
        P("rows", None, "comp", None, None),
        P("rows", None, "comp", None, None),
        P(),
        P(),
        P("rows", "comp", None, None, None, None, None),
        P("rows", None),
        P("rows", None, "comp"),
        P("rows", None, "comp"),
    )
    return jax.shard_map(
        shards,
        mesh=mesh,
        in_specs=placed,
        out_specs=(
            P("rows", None, "comp", None, None),
            P("rows", None, "comp", None, None),
            P("rows", None, "comp", None, None),
            P("rows", None, "comp", None, None),
            P(),
            P(),
            P("rows", None, None, None, "comp", None),
        ),
        check_vma=False,
    )
```

profile of v0, /device:TPU:0, one launch (start us, length us, event | category | flops | bytes accessed | tf_op | source)
XLA Modules:
  0.0 447.1 jit_solution(5496281987982016223)
XLA Ops:
  9.8 2.4 select_bitcast_fusion.1
  31.5 10.3 %fusion.10 = f32[128,2,1,64]{3,2,1,0:T(1,128)} fusion(f32[128,2,64]{0,2,1:T(8,128)} %exponential-minus-one_negate_fusion.1, f32[128,2,64]{0,2,1:T(8,128)S(1)} %copy.149, f32[128,2,64]{2,1,0:T(2,128)} %copy-done.29, pred[128,128]{1,0:T(8,128)(4,1)S(1)} %iota_compare_fusion, bf16[128,2,128,1]{2,0,1,3:T(8,128)(2,1)S(1)} %bitcast.438), kind=kOutput, calls=%fused_computation.19 | convolution fusion | flops 33554432 | bytes 344064 | tf_op jit(solution)/shard_map/transpose(jvp(thm,tjhm->thj))/dot_general | solution.py:40
  41.8 10.8 %multiply_reduce_fusion.3 = (f32[128,2,64]{2,1,0:T(2,128)}, f32[128,2,64]{2,1,0:T(2,128)}) fusion(f32[128,2,128]{2,1,0:T(2,128)S(1)} %copy-done.39, f32[128,2,64]{0,2,1:T(8,128)S(1)} %copy-done.46, f32[128,2,64]{0,2,1:T(8,128)S(1)} %copy.149, f32[128,2,64]{2,1,0:T(2,128)S(1)} %copy-done.30, pred[128,128]{1,0:T(8,128)(4,1)S(1)} %iota_compare_fusion, ...), kind=kLoop, calls=%fused_computation.5 | loop fusion | flops 25133056 | bytes 802816
  56.2 1.6 copy.215
  57.8 1.6 copy.236
  61.2 1.7 copy.191
  62.9 9.9 %fusion.4 = f32[128,2,1,64]{3,2,1,0:T(1,128)} fusion(f32[128,2,64]{0,2,1:T(8,128)} %exponential-minus-one_negate_fusion, f32[128,2,64]{0,2,1:T(8,128)S(1)} %copy.164, f32[128,2,64]{2,1,0:T(2,128)} %copy-done.25, pred[128,128]{1,0:T(8,128)(4,1)S(1)} %iota_compare_fusion, bf16[128,2,128,1]{2,0,1,3:T(8,128)(2,1)} %bitcast.437), kind=kOutput, calls=%fused_computation.14 | convolution fusion | flops 33554432 | bytes 344064 | tf_op jit(solution)/shard_map/transpose(jvp(thm,tjhm->thj))/dot_general | solution.py:40
  74.4 35.1 %all-reduce.16.cloned.1.call-done = (f32[2,2,64,640]{3,2,1,0:T(8,128)}, f32[2,2,64,640]{3,2,1,0:T(8,128)}) async-done(((f32[2,2,64,640]{3,2,1,0:T(8,128)}, f32[2,2,64,640]{3,2,1,0:T(8,128)}), (f32[2,2,64,640]{3,2,1,0:T(8,128)}, f32[2,2,64,640]{3,2,1,0:T(8,128)})) %all-reduce.16.cloned.1.call-update) | async-done | bytes 1310736 | tf_op jit(solution)/shard_map/psum | solution.py:9
  109.6 2.0 fusion.162
  112.1 1.9 fusion.160
  117.5 1.6 copy.267
  120.6 1.6 multiply_reduce_fusion.6
  124.3 1.6 copy.269
  126.8 12.0 %multiply_reduce_fusion.2 = (f32[128,2,128]{2,1,0:T(2,128)}, f32[128,2,128]{2,1,0:T(2,128)}) fusion(f32[128,2,64]{2,1,0:T(2,128)} %copy.267, f32[128,2,64]{0,2,1:T(8,128)} %exponential-minus-one_negate_fusion.1, f32[128,2,64]{0,2,1:T(8,128)S(1)} %copy.149, f32[128,2,64]{2,1,0:T(2,128)} %copy-done.29, pred[128,128]{1,0:T(8,128)(4,1)} %copy-done.48, ...), kind=kLoop, calls=%fused_computation.4 | loop fusion | flops 25100288 | bytes 802816
  138.8 20.1 %fusion.13 = (f32[128,2,64]{0,2,1:T(8,128)}, f32[128,2,64]{2,1,0:T(2,128)}, f32[128,2,64]{0,2,1:T(8,128)}, f32[128,2,64]{0,2,1:T(8,128)}, f32[128,2,64]{2,1,0:T(2,128)}, /*index=5*/f32[128,2,64]{0,2,1:T(8,128)}) fusion(f32[128,2,64]{2,1,0:T(2,128)S(1)} %copy-done.33, f32[128,2,128]{2,1,0:T(2,128)S(1)} %copy-done.40, f32[128,2,64]{2,1,0:T(2,128)S(1)} %copy-done.34, ...), kind=kLoop, calls=%fused_computation.21 | loop fusion | flops 58621952 | bytes 1589248 | tf_op jit(solution)/shard_map/transpose(jvp())/reduce_sum | solution.py:23
  158.9 1.6 copy.188
  160.5 1.7 fusion.132
  162.2 1.6 copy.189
  163.8 2.6 reduce_window_sum.41
  166.4 1.6 copy.190
  170.9 1.6 copy.195
  172.5 1.7 fusion.124
  174.2 1.6 copy.196
  175.7 2.6 reduce_window_sum.43
  178.3 1.6 copy.197
  179.9 1.8 fusion.156
  182.2 31.7 %all-reduce.5 = f32[128]{0:T(128)} all-reduce(f32[128]{0:T(128)} %negate_add_fusion), channel_id=3, replica_groups=mesh['comp'=16,'rows'=2] {'comp'}, use_global_device_ids=true, to_apply=%region_22.24.clone | all-reduce | flops 128 | bytes 1024
  216.9 2.8 copy.256
  221.1 9.9 %fusion.8 = bf16[128,2,1,128]{3,2,1,0:T(2,128)(2,1)} fusion(f32[128,2,64,1]{2,3,1,0:T(1,128)} %copy.248, f32[128,2,64]{0,2,1:T(8,128)} %exponential-minus-one_negate_fusion.1, f32[128,2,64]{0,2,1:T(8,128)S(1)} %copy.149, f32[128,2,64]{2,1,0:T(2,128)} %copy-done.29, pred[128,128]{1,0:T(8,128)(4,1)} %copy-done.48), kind=kOutput, calls=%fused_computation.18 | convolution fusion | flops 33554432 | bytes 344064 | tf_op jit(solution)/shard_map/jvp(thm,tjhm->thj)/dot_general | solution.py:40
  231.0 5.5 %psum.31 = f32[8]{0:T(128)} all-reduce(f32[8]{0:T(128)} %dynamic-slice.2), channel_id=1, replica_groups=mesh['comp'=16,'rows'=2] {'rows'}, use_global_device_ids=true, to_apply=%region_23.25 | all-reduce | flops 8 | bytes 64 | tf_op jit(solution)/shard_map/psum | solution.py:114
  236.5 1.9 convolution_convert_fusion.5
  238.4 1.9 copy.182
  241.0 1.7 copy.222
  242.7 1.9 fusion.41
  244.6 1.9 copy.179
  253.2 1.6 fusion.84
  254.7 20.8 %reduce-scatter.5.cloned.1.call-done = f32[160,128]{1,0:T(8,128)} async-done(((f32[2560,128]{1,0:T(8,128)}), f32[160,128]{1,0:T(8,128)}) %reduce-scatter.5.cloned.1.call-update) | async-done | bytes 81936
  275.6 1.6 copy.257
  277.3 2.2 pad_maximum_fusion
  282.2 1.7 fusion.85
  284.4 14.7 %all-reduce.12.cloned.1.call-done = f32[160,128]{0,1:T(8,128)} async-done(((f32[160,128]{0,1:T(8,128)}), f32[160,128]{0,1:T(8,128)}) %all-reduce.12.cloned.1.call-update) | async-done | bytes 81936 | tf_op jit(solution)/shard_map/psum | solution.py:114
  299.1 1.6 copy.198
  303.6 8.2 %fusion.2 = bf16[128,2,1,128]{3,2,1,0:T(2,128)(2,1)S(1)} fusion(f32[128,2,64,1]{2,3,1,0:T(1,128)S(1)} %copy-done.32, f32[128,2,64]{0,2,1:T(8,128)S(1)} %copy-done.45, f32[128,2,64]{0,2,1:T(8,128)S(1)} %copy.164, f32[128,2,64]{2,1,0:T(2,128)S(1)} %copy-done.28, pred[128,128]{1,0:T(8,128)(4,1)S(1)} %copy-done.50), kind=kOutput, calls=%fused_computation.13 | convolution fusion | flops 33554432 | bytes 344064 | tf_op jit(solution)/shard_map/jvp(thm,tjhm->thj)/dot_general | solution.py:40
  312.6 33.3 %all-reduce.4 = f32[128]{0:T(128)} all-reduce(f32[128]{0:T(128)S(1)} %dynamic-update-slice), channel_id=1, replica_groups=mesh['comp'=16,'rows'=2] {'comp'}, use_global_device_ids=true, to_apply=%add.4 | all-reduce | flops 128 | bytes 1024
  349.0 48.3 %all-reduce.14.cloned.1.call-done = f32[2,2,2,64,640]{4,3,2,1,0:T(8,128)} async-done(((f32[2,2,2,64,640]{4,3,2,1,0:T(8,128)}), f32[2,2,2,64,640]{4,3,2,1,0:T(8,128)}) %all-reduce.14.cloned.1.call-update) | async-done | bytes 1310736
  397.3 1.6 dynamic-slice_bitcast_fusion
  398.9 39.0 %all-gather.2.cloned.1.call-done = f32[2560,128]{1,0:T(8,128)} async-done(((f32[160,128]{1,0:T(8,128)}), f32[2560,128]{1,0:T(8,128)}) %all-gather.2.cloned.1.call-update) | async-done | bytes 1310736 | tf_op jit(solution)/shard_map/all_gather | solution.py:116
  437.9 2.5 copy.288
  (215 shorter events, 59.0 us)
Async XLA Ops:
  7.2 5.2 %copy-start = (bf16[2560,128]{1,0:T(8,128)(2,1)S(1)}, bf16[2560,128]{1,0:T(8,128)(2,1)}, u32[]{:S(2)}) copy-start(bf16[2560,128]{1,0:T(8,128)(2,1)} %param.17) | copy-start | bytes 1966084
  7.2 102.4 %all-reduce.16.cloned.1.call-start = ((), (), s32[]{:S(2)}) async-start(), calls=%async_computation.5 | async-start | bytes 2621440 | tf_op jit(solution)/shard_map/psum | solution.py:9
  12.3 263.3 %reduce-scatter.5.cloned.1.call-start = ((), (), s32[]{:S(2)}) async-start(), calls=%async_computation.3 | async-start | bytes 1392640
  13.6 49.3 %copy-start.48 = (pred[128,128]{1,0:T(8,128)(4,1)}, pred[128,128]{1,0:T(8,128)(4,1)S(1)}, u32[]{:S(2)}) copy-start(pred[128,128]{1,0:T(8,128)(4,1)S(1)} %iota_compare_fusion) | copy-start | bytes 49156
  14.6 2.6 copy-start.57
  14.6 3.2 copy-start.58
  15.4 4.1 copy-start.16
  20.9 2.4 copy-start.18
  23.3 1.8 copy-start.19
  28.9 2.5 copy-start.55
  30.1 22.5 %copy-start.53 = (f32[128]{0:T(128)}, f32[128]{0:T(128)S(1)}, u32[]{:S(2)}) copy-start(f32[128]{0:T(128)S(1)} %fusion.147) | copy-start | bytes 1540
  31.5 10.3 %copy-start.26 = (f32[128,2,64]{2,1,0:T(2,128)S(1)}, f32[128,2,64]{2,1,0:T(2,128)}, u32[]{:S(2)}) copy-start(f32[128,2,64]{2,1,0:T(2,128)} %copy-done.25) | copy-start | bytes 196612
  31.5 10.3 %copy-start.30 = (f32[128,2,64]{2,1,0:T(2,128)S(1)}, f32[128,2,64]{2,1,0:T(2,128)}, u32[]{:S(2)}) copy-start(f32[128,2,64]{2,1,0:T(2,128)} %copy-done.29) | copy-start | bytes 196612
  31.5 10.3 %copy-start.37 = (f32[128,2,128]{2,1,0:T(2,128)S(1)}, f32[128,2,128]{2,1,0:T(2,128)}, u32[]{:S(2)}) copy-start(f32[128,2,128]{2,1,0:T(2,128)} %copy.268) | copy-start | bytes 393220
  31.5 10.3 %copy-start.39 = (f32[128,2,128]{2,1,0:T(2,128)S(1)}, f32[128,2,128]{2,1,0:T(2,128)}, u32[]{:S(2)}) copy-start(f32[128,2,128]{2,1,0:T(2,128)} %copy.266) | copy-start | bytes 393220
  31.5 10.3 %copy-start.43 = (f32[128,2,64]{0,2,1:T(8,128)S(1)}, f32[128,2,64]{0,2,1:T(8,128)}, u32[]{:S(2)}) copy-start(f32[128,2,64]{0,2,1:T(8,128)} %exponential-minus-one_negate_fusion) | copy-start | bytes 196612
  31.5 10.3 %copy-start.46 = (f32[128,2,64]{0,2,1:T(8,128)S(1)}, f32[128,2,64]{0,2,1:T(8,128)}, u32[]{:S(2)}) copy-start(f32[128,2,64]{0,2,1:T(8,128)} %exponential-minus-one_negate_fusion.1) | copy-start | bytes 196612
  41.8 10.8 %copy-start.12 = (bf16[1,1,1,128,1280]{3,4,2,1,0:T(8,128)(2,1)S(1)}, bf16[1,1,1,128,1280]{3,4,2,1,0:T(8,128)(2,1)}, u32[]{:S(2)}) copy-start(bf16[1,1,1,128,1280]{3,4,2,1,0:T(8,128)(2,1)} %copy.263) | copy-start | bytes 983044
  61.2 52.9 %copy-start.3 = (f32[128,2,1,64]{0,3,1,2:T(8,128)}, f32[128,2,1,64]{0,3,1,2:T(8,128)S(1)}, u32[]{:S(2)}) copy-start(f32[128,2,1,64]{0,3,1,2:T(8,128)S(1)} %copy.207) | copy-start | bytes 196612
  73.8 46.8 %copy-start.2 = (f32[128,2,1,64]{0,3,1,2:T(8,128)}, f32[128,2,1,64]{0,3,1,2:T(8,128)S(1)}, u32[]{:S(2)}) copy-start(f32[128,2,1,64]{0,3,1,2:T(8,128)S(1)} %copy.228) | copy-start | bytes 196612
  109.6 4.5 %copy-start.6 = (f32[2,2,64,640]{3,2,1,0:T(8,128)S(1)}, f32[2,2,64,640]{3,2,1,0:T(8,128)}, u32[]{:S(2)}) copy-start(f32[2,2,64,640]{3,2,1,0:T(8,128)} %get-tuple-element.57) | copy-start | bytes 1966084
  111.5 6.0 %copy-start.4 = (f32[128,2,64]{0,2,1:T(8,128)}, f32[128,2,64]{0,2,1:T(8,128)S(1)}, u32[]{:S(2)}) copy-start(f32[128,2,64]{0,2,1:T(8,128)S(1)} %get-tuple-element.65) | copy-start | bytes 196612
  114.0 1.9 copy-start.5
  115.4 2.1 copy-start.14
  126.7 12.1 %copy-start.27 = (f32[128,2,64]{2,1,0:T(2,128)S(1)}, f32[128,2,64]{2,1,0:T(2,128)}, u32[]{:S(2)}) copy-start(f32[128,2,64]{2,1,0:T(2,128)} %copy-done.25) | copy-start | bytes 196612
  126.7 12.1 %copy-start.31 = (f32[128,2,64]{2,1,0:T(2,128)S(1)}, f32[128,2,64]{2,1,0:T(2,128)}, u32[]{:S(2)}) copy-start(f32[128,2,64]{2,1,0:T(2,128)} %copy-done.29) | copy-start | bytes 196612
  126.7 12.1 %copy-start.33 = (f32[128,2,64]{2,1,0:T(2,128)S(1)}, f32[128,2,64]{2,1,0:T(2,128)}, u32[]{:S(2)}) copy-start(f32[128,2,64]{2,1,0:T(2,128)} %copy.267) | copy-start | bytes 196612
  126.7 12.1 %copy-start.34 = (f32[128,2,64]{2,1,0:T(2,128)S(1)}, f32[128,2,64]{2,1,0:T(2,128)}, u32[]{:S(2)}) copy-start(f32[128,2,64]{2,1,0:T(2,128)} %copy.185) | copy-start | bytes 196612
  126.7 12.1 %copy-start.35 = (f32[128,2,64]{2,1,0:T(2,128)S(1)}, f32[128,2,64]{2,1,0:T(2,128)}, u32[]{:S(2)}) copy-start(f32[128,2,64]{2,1,0:T(2,128)} %copy.269) | copy-start | bytes 196612
  126.7 12.1 %copy-start.36 = (f32[128,2,64]{2,1,0:T(2,128)S(1)}, f32[128,2,64]{2,1,0:T(2,128)}, u32[]{:S(2)}) copy-start(f32[128,2,64]{2,1,0:T(2,128)} %copy.192) | copy-start | bytes 196612
  126.7 12.1 %copy-start.38 = (f32[128,2,128]{2,1,0:T(2,128)S(1)}, f32[128,2,128]{2,1,0:T(2,128)}, u32[]{:S(2)}) copy-start(f32[128,2,128]{2,1,0:T(2,128)} %copy.268) | copy-start | bytes 393220
  126.7 12.1 %copy-start.40 = (f32[128,2,128]{2,1,0:T(2,128)S(1)}, f32[128,2,128]{2,1,0:T(2,128)}, u32[]{:S(2)}) copy-start(f32[128,2,128]{2,1,0:T(2,128)} %copy.266) | copy-start | bytes 393220
  126.7 12.1 %copy-start.41 = (f32[128,2,128]{2,1,0:T(2,128)S(1)}, f32[128,2,128]{2,1,0:T(2,128)}, u32[]{:S(2)}) copy-start(f32[128,2,128]{2,1,0:T(2,128)} %copy.184) | copy-start | bytes 393220
  126.7 12.1 %copy-start.42 = (f32[128,2,128]{2,1,0:T(2,128)S(1)}, f32[128,2,128]{2,1,0:T(2,128)}, u32[]{:S(2)}) copy-start(f32[128,2,128]{2,1,0:T(2,128)} %copy.191) | copy-start | bytes 393220
  126.7 12.1 %copy-start.44 = (f32[128,2,64]{0,2,1:T(8,128)S(1)}, f32[128,2,64]{0,2,1:T(8,128)}, u32[]{:S(2)}) copy-start(f32[128,2,64]{0,2,1:T(8,128)} %exponential-minus-one_negate_fusion) | copy-start | bytes 196612
  126.8 12.1 %copy-start.47 = (f32[128,2,64]{0,2,1:T(8,128)S(1)}, f32[128,2,64]{0,2,1:T(8,128)}, u32[]{:S(2)}) copy-start(f32[128,2,64]{0,2,1:T(8,128)} %exponential-minus-one_negate_fusion.1) | copy-start | bytes 196612
  126.8 12.1 %copy-start.49 = (pred[128,128]{1,0:T(8,128)(4,1)S(1)}, pred[128,128]{1,0:T(8,128)(4,1)}, u32[]{:S(2)}) copy-start(pred[128,128]{1,0:T(8,128)(4,1)} %copy-done.48) | copy-start | bytes 49156
  213.9 1.5 copy-start.9
  213.9 1.6 copy-start.22
  219.7 79.4 %all-reduce.12.cloned.1.call-start = ((), (), s32[]{:S(2)}) async-start(), calls=%async_computation.1 | async-start | bytes 262144 | tf_op jit(solution)/shard_map/psum | solution.py:114
  246.4 3.6 copy-start.56
  247.4 3.5 copy-start.54
  277.2 120.1 %all-reduce.14.cloned.1.call-start = ((), (), s32[]{:S(2)}) async-start(), calls=%async_computation.4 | async-start | bytes 2621440
  279.6 2.6 copy-start.21
  279.6 158.3 %all-gather.2.cloned.1.call-start = ((), (), s32[]{:S(2)}) async-start(), calls=%async_computation.2 | async-start | bytes 1392640 | tf_op jit(solution)/shard_map/all_gather | solution.py:116
  300.8 1.6 copy-start.11
  311.8 34.1 %copy-start.24 = (f32[128,128]{0,1:T(8,128)S(1)}, f32[128,128]{0,1:T(8,128)}, u32[]{:S(2)}) copy-start(f32[128,128]{0,1:T(8,128)} %get-tuple-element.59) | copy-start | bytes 196612
  311.9 34.5 %copy-start.23 = (f32[128,128]{0,1:T(8,128)S(1)}, f32[128,128]{0,1:T(8,128)}, u32[]{:S(2)}) copy-start(f32[128,128]{0,1:T(8,128)} %get-tuple-element.107) | copy-start | bytes 196612
  (18 other events, 19.6 us)
Sparse Core Ops, SparseCore 0:
  12.4 97.0 all-reduce.15
  219.8 55.7 reduce-scatter.4
  278.4 20.6 all-reduce.11
  303.0 94.2 all-reduce.13
  399.5 38.3 all-gather.1
where the time goes:
time: 453 us; the launch traced here: 447 us
  waiting for transfers between devices  158 us (35%)
  other arithmetic  76.4 us (17%)
  blocking collectives  70.6 us (16%)
  matrix products  64.4 us (14%)
  local copies, waits for them, and re-layouts  59.1 us (13%)
  between operations  18 us (4%)
    unnamed x7, waiting for transfers between devices  69.2 us
    unnamed x2, blocking collectives  65.1 us
    all_gather x1, waiting for transfers between devices, shards(): lax.all_gather(weight_block, 'comp', axis=0, tiled=True)  39 us
    dot_general x4, matrix products, slot_forward(): jnp.einsum('thm,tjhm->thj', slot_probabilities, reach, precision=highest_...  38.3 us
    psum x1, waiting for transfers between devices, broadcast(): return lax.psum(block, axis)  35.1 us
    unnamed x140, local copies, waits for them, and re-layouts  24.1 us
    unnamed x3, other arithmetic  23.9 us
    reduce_sum x1, other arithmetic, slot_forward(): between = running[:, None] - running[None, :]  20.1 us
  transfers between devices with their start and end apart: 5, of which 5 were waited for; matrix products, arithmetic and copies ran while one was open for 24% of the time, Pallas kernels for 0%

commit v1 on v0

--- a/solution.py
+++ b/solution.py
@@ -6,7 +6,7 @@
 
 def broadcast(block, axis, holder):
     block = jnp.where(lax.axis_index(axis) == holder, block, jnp.zeros_like(block))
-    return lax.psum(block, axis)
+    return jnp.sum(lax.all_gather(block, axis), axis=0)
 
 
 def slot_forward(gates, queries, keys_in, values_in, anchor_point):

time: 453 us -> 551 us (1.22)
  waiting for transfers between devices: 158 us -> 231 us
  other arithmetic: 76.4 us -> 102 us
  local copies, waits for them, and re-layouts: 59.1 us -> 53.5 us
    all_gather x0 -> x2, waiting for transfers between devices: none -> 113 us  [broadcast(): return jnp.sum(lax.all_gather(block, axis), axis=0)]
    psum x1 -> x0, waiting for transfers between devices: 35.1 us -> none  [broadcast(): return lax.psum(block, axis)]
    reduce_sum x1, other arithmetic: 20.1 us -> 33.7 us  [slot_forward(): between = running[:, None] - running[None, :]]
    reduce_sum x0 -> x2, other arithmetic: none -> 9.9 us  [broadcast(): return jnp.sum(lax.all_gather(block, axis), axis=0)]
    unnamed x140 -> x84, local copies, waits for them, and re-layouts: 24.1 us -> 19 us
    unnamed x7 -> x8, waiting for transfers between devices: 69.2 us -> 65.2 us
  transfers between devices with their start and end apart: 5 -> 6, of which waited for: 5 -> 6; matrix products, arithmetic and copies ran while one was open for 24% -> 22% of each run, Pallas kernels for 0% -> 0%
where the time goes in v1:
time: 551 us; the launch traced here: 545 us
  waiting for transfers between devices  231 us (42%)
  other arithmetic  102 us (19%)
  blocking collectives  70.4 us (13%)
  matrix products  69.9 us (13%)
  local copies, waits for them, and re-layouts  53.5 us (10%)
  between operations  18.2 us (3%)
    all_gather x2, waiting for transfers between devices, broadcast(): return jnp.sum(lax.all_gather(block, axis), axis=0)  113 us
    unnamed x8, waiting for transfers between devices  65.2 us
    unnamed x2, blocking collectives  64.9 us
    all_gather x1, waiting for transfers between devices, shards(): lax.all_gather(weight_block, 'comp', axis=0, tiled=True)  39 us
    dot_general x4, matrix products, slot_forward(): jnp.einsum('thm,tjhm->thj', slot_probabilities, reach, precision=highest_...  37.8 us
    reduce_sum x1, other arithmetic, slot_forward(): between = running[:, None] - running[None, :]  33.7 us
    unnamed x3, other arithmetic  23.4 us
    unnamed x84, local copies, waits for them, and re-layouts  19 us
  transfers between devices with their start and end apart: 6, of which 6 were waited for; matrix products, arithmetic and copies ran while one was open for 22% of the time, Pallas kernels for 0%

profile of v1, /device:TPU:0, one launch (start us, length us, event | category | flops | bytes accessed | tf_op | source)
XLA Modules:
  0.0 545.3 jit_solution(12590343212639843730)
XLA Ops:
  9.9 2.4 slice_select_fusion.1
  15.9 2.1 negate_multiply_fusion
  18.3 2.1 negate_multiply_fusion.1
  23.8 10.5 %multiply_reduce_fusion.3 = (f32[128,2,64]{2,1,0:T(2,128)S(1)}, f32[128,2,64]{2,1,0:T(2,128)S(1)}) fusion(f32[128,2,128]{2,1,0:T(2,128)S(1)} %copy.266, f32[128,2,64]{0,2,1:T(8,128)S(1)} %exponential-minus-one_negate_fusion.1, f32[128,2,64]{0,2,1:T(8,128)S(1)} %copy.149, f32[128,2,64]{2,1,0:T(2,128)S(1)} %fusion.172, ...), kind=kLoop, calls=%fused_computation.5 | loop fusion | flops 25133056 | bytes 802816
  38.7 2.0 slice_convert_fusion.1
  48.0 9.3 %fusion.10 = f32[128,2,1,64]{3,2,1,0:T(1,128)S(1)} fusion(f32[128,2,64]{0,2,1:T(8,128)} %copy-done.24, f32[128,2,64]{0,2,1:T(8,128)S(1)} %copy.149, f32[128,2,64]{2,1,0:T(2,128)S(1)} %fusion.172, pred[128,128]{1,0:T(8,128)(4,1)S(1)} %iota_compare_fusion, bf16[128,2,128,1]{2,0,1,3:T(8,128)(2,1)S(1)} %bitcast.433), kind=kOutput, calls=%fused_computation.19 | convolution fusion | flops 33554432 | bytes 344064 | tf_op jit(solution)/shard_map/transpose(jvp(thm,tjhm->thj))/dot_general | solution.py:40
  61.1 9.3 %fusion.4 = f32[128,2,1,64]{3,2,1,0:T(1,128)S(1)} fusion(f32[128,2,64]{0,2,1:T(8,128)} %copy-done.23, f32[128,2,64]{0,2,1:T(8,128)S(1)} %copy.164, f32[128,2,64]{2,1,0:T(2,128)} %copy-done.18, pred[128,128]{1,0:T(8,128)(4,1)S(1)} %iota_compare_fusion, bf16[128,2,128,1]{2,0,1,3:T(8,128)(2,1)S(1)} %bitcast.434), kind=kOutput, calls=%fused_computation.14 | convolution fusion | flops 33554432 | bytes 344064 | tf_op jit(solution)/shard_map/transpose(jvp(thm,tjhm->thj))/dot_general | solution.py:40
  71.8 31.0 %all-gather.10.cloned.1.call-done = f32[16,1,1,2,2,64,640]{6,5,4,3,2,1,0:T(8,128)} async-done(((f32[1,1,1,2,2,64,640]{6,5,4,3,2,1,0:T(8,128)}), f32[16,1,1,2,2,64,640]{6,5,4,3,2,1,0:T(8,128)}) %all-gather.10.cloned.1.call-update) | async-done | bytes 10485776 | tf_op jit(solution)/shard_map/all_gather | solution.py:9
  102.8 4.5 reduce_sum.127
  107.3 1.8 fusion.162
  109.7 81.7 %all-gather.8.cloned.1.call-done = f32[16,1,1,2,2,64,640]{6,5,4,3,2,1,0:T(8,128)} async-done(((f32[1,1,1,2,2,64,640]{6,5,4,3,2,1,0:T(8,128)}), f32[16,1,1,2,2,64,640]{6,5,4,3,2,1,0:T(8,128)}) %all-gather.8.cloned.1.call-update) | async-done | bytes 10485776 | tf_op jit(solution)/shard_map/all_gather | solution.py:9
  191.4 5.4 reduce_sum.121
  196.8 1.9 fusion.160
  201.6 1.6 copy.267
  208.3 1.6 copy.269
  210.7 11.8 %multiply_reduce_fusion.2 = (f32[128,2,128]{2,1,0:T(2,128)}, f32[128,2,128]{2,1,0:T(2,128)}) fusion(f32[128,2,64]{2,1,0:T(2,128)} %copy.267, f32[128,2,64]{0,2,1:T(8,128)} %copy-done.24, f32[128,2,64]{0,2,1:T(8,128)S(1)} %copy.149, f32[128,2,64]{2,1,0:T(2,128)} %copy-done.19, pred[128,128]{1,0:T(8,128)(4,1)} %copy-done.25, f32[128,2,64]{0,2,1:T(8,128)} %copy-done.23, ...), kind=kLoop, calls=%fused_computation.4 | loop fusion | flops 25100288 | bytes 802816
  222.4 33.7 %fusion.13 = (f32[128,2,64]{0,2,1:T(8,128)}, f32[128,2,64]{2,1,0:T(2,128)}, f32[128,2,64]{0,2,1:T(8,128)}, f32[128,2,64]{0,2,1:T(8,128)}, f32[128,2,64]{2,1,0:T(2,128)}, /*index=5*/f32[128,2,64]{0,2,1:T(8,128)}) fusion(f32[128,2,64]{2,1,0:T(2,128)} %copy.267, f32[128,2,128]{2,1,0:T(2,128)} %copy-done.22, f32[128,2,64]{2,1,0:T(2,128)} %copy.185, ...), kind=kLoop, calls=%fused_computation.21 | loop fusion | flops 58621952 | bytes 1589248 | tf_op jit(solution)/shard_map/transpose(jvp())/reduce_sum | solution.py:23
  256.2 1.6 copy.188
  257.8 1.7 fusion.132
  259.4 1.6 copy.189
  261.0 2.6 reduce_window_sum.41
  263.6 1.6 copy.190
  268.1 1.6 copy.195
  269.7 1.7 fusion.124
  273.0 2.6 reduce_window_sum.43
  277.1 1.8 fusion.156
  279.4 31.5 %all-reduce.5 = f32[128]{0:T(128)} all-reduce(f32[128]{0:T(128)} %negate_add_fusion), channel_id=5, replica_groups=mesh['comp'=16,'rows'=2] {'comp'}, use_global_device_ids=true, to_apply=%region_22.24.clone | all-reduce | flops 128 | bytes 1024
  312.4 2.5 fusion.36
  314.9 2.8 copy.256
  319.0 9.9 %fusion.8 = bf16[128,2,1,128]{3,2,1,0:T(2,128)(2,1)} fusion(f32[128,2,64,1]{2,3,1,0:T(1,128)} %copy.248, f32[128,2,64]{0,2,1:T(8,128)} %copy-done.24, f32[128,2,64]{0,2,1:T(8,128)S(1)} %copy.149, f32[128,2,64]{2,1,0:T(2,128)} %copy-done.19, pred[128,128]{1,0:T(8,128)(4,1)} %copy-done.25), kind=kOutput, calls=%fused_computation.18 | convolution fusion | flops 33554432 | bytes 344064 | tf_op jit(solution)/shard_map/jvp(thm,tjhm->thj)/dot_general | solution.py:40
  328.9 5.5 %psum.15 = f32[8]{0:T(128)} all-reduce(f32[8]{0:T(128)} %dynamic-slice.2), channel_id=1, replica_groups=mesh['comp'=16,'rows'=2] {'rows'}, use_global_device_ids=true, to_apply=%region_23.25 | all-reduce | flops 8 | bytes 64 | tf_op jit(solution)/shard_map/psum | solution.py:114
  334.4 1.9 convolution_convert_fusion.5
  336.3 1.9 copy.182
  338.9 1.7 copy.222
  340.5 1.9 fusion.41
  342.4 1.9 copy.179
  349.5 1.6 convolution_bitcast_fusion.1
  352.3 2.5 fusion.84
  354.8 18.8 %reduce-scatter.5.cloned.1.call-done = f32[160,128]{1,0:T(8,128)} async-done(((f32[2560,128]{1,0:T(8,128)}), f32[160,128]{1,0:T(8,128)}) %reduce-scatter.5.cloned.1.call-update) | async-done | bytes 81936
  373.6 1.6 copy.257
  375.3 2.4 pad_maximum_fusion
  382.6 14.3 %all-reduce.10.cloned.1.call-done = f32[160,128]{0,1:T(8,128)} async-done(((f32[160,128]{0,1:T(8,128)}), f32[160,128]{0,1:T(8,128)}) %all-reduce.10.cloned.1.call-update) | async-done | bytes 81936 | tf_op jit(solution)/shard_map/psum | solution.py:114
  397.0 1.6 copy.198
  403.4 9.3 %fusion.2 = bf16[128,2,1,128]{3,2,1,0:T(2,128)(2,1)S(1)} fusion(f32[128,2,64,1]{2,3,1,0:T(1,128)} %copy.250, f32[128,2,64]{0,2,1:T(8,128)} %copy-done.23, f32[128,2,64]{0,2,1:T(8,128)S(1)} %copy.164, f32[128,2,64]{2,1,0:T(2,128)} %copy-done.18, pred[128,128]{1,0:T(8,128)(4,1)S(1)} %copy-done.26), kind=kOutput, calls=%fused_computation.13 | convolution fusion | flops 33554432 | bytes 344064 | tf_op jit(solution)/shard_map/jvp(thm,tjhm->thj)/dot_general | solution.py:40
  413.3 33.4 %all-reduce.4 = f32[128]{0:T(128)} all-reduce(f32[128]{0:T(128)S(1)} %dynamic-update-slice), channel_id=1, replica_groups=mesh['comp'=16,'rows'=2] {'comp'}, use_global_device_ids=true, to_apply=%add.4 | all-reduce | flops 128 | bytes 1024
  449.5 45.7 %all-reduce.12.cloned.1.call-done = f32[2,2,2,64,640]{4,3,2,1,0:T(8,128)} async-done(((f32[2,2,2,64,640]{4,3,2,1,0:T(8,128)}), f32[2,2,2,64,640]{4,3,2,1,0:T(8,128)}) %all-reduce.12.cloned.1.call-update) | async-done | bytes 1310736
  496.8 39.0 %all-gather.6.cloned.1.call-done = f32[2560,128]{1,0:T(8,128)} async-done(((f32[160,128]{1,0:T(8,128)}), f32[2560,128]{1,0:T(8,128)}) %all-gather.6.cloned.1.call-update) | async-done | bytes 1310736 | tf_op jit(solution)/shard_map/all_gather | solution.py:116
  535.8 2.5 copy.286
  (164 shorter events, 63.6 us)
Async XLA Ops:
  7.2 8.7 %copy-start = (bf16[2560,128]{1,0:T(8,128)(2,1)S(1)}, bf16[2560,128]{1,0:T(8,128)(2,1)}, u32[]{:S(2)}) copy-start(bf16[2560,128]{1,0:T(8,128)(2,1)} %param.17) | copy-start | bytes 1966084
  7.2 13.6 %copy-start.12 = (bf16[1,2,1,128,1280]{4,3,2,1,0:T(8,128)(2,1)S(1)}, bf16[1,2,1,128,1280]{4,3,2,1,0:T(8,128)(2,1)}, u32[]{:S(2)}) copy-start(bf16[1,2,1,128,1280]{4,3,2,1,0:T(8,128)(2,1)} %param.13) | copy-start | bytes 1966084
  7.2 14.3 %copy-start.13 = (bf16[1,2,1,128,1280]{4,3,2,1,0:T(8,128)(2,1)S(1)}, bf16[1,2,1,128,1280]{4,3,2,1,0:T(8,128)(2,1)}, u32[]{:S(2)}) copy-start(bf16[1,2,1,128,1280]{4,3,2,1,0:T(8,128)(2,1)} %param.14) | copy-start | bytes 1966084
  7.2 95.6 %all-gather.10.cloned.1.call-start = ((), (), s32[]{:S(2)}) async-start(), calls=%async_computation.4 | async-start | bytes 11141120 | tf_op jit(solution)/shard_map/all_gather | solution.py:9
  12.4 179.0 %all-gather.8.cloned.1.call-start = ((), (), s32[]{:S(2)}) async-start(), calls=%async_computation.3 | async-start | bytes 11141120 | tf_op jit(solution)/shard_map/all_gather | solution.py:9
  13.1 360.5 %reduce-scatter.5.cloned.1.call-start = ((), (), s32[]{:S(2)}) async-start(), calls=%async_computation.5 | async-start | bytes 1392640
  18.2 16.1 %copy-start.18 = (f32[128,2,64]{2,1,0:T(2,128)}, f32[128,2,64]{2,1,0:T(2,128)S(1)}, u32[]{:S(2)}) copy-start(f32[128,2,64]{2,1,0:T(2,128)S(1)} %fusion.173) | copy-start | bytes 196612
  20.4 0.6 copy-start.20
  20.7 27.4 %copy-start.19 = (f32[128,2,64]{2,1,0:T(2,128)}, f32[128,2,64]{2,1,0:T(2,128)S(1)}, u32[]{:S(2)}) copy-start(f32[128,2,64]{2,1,0:T(2,128)S(1)} %fusion.172) | copy-start | bytes 196612
  21.7 20.2 %copy-start.1 = (bf16[1,1,1,128,1280]{3,4,2,1,0:T(8,128)(2,1)}, bf16[1,1,1,128,1280]{3,4,2,1,0:T(8,128)(2,1)S(1)}, u32[]{:S(2)}) copy-start(bf16[1,1,1,128,1280]{3,4,2,1,0:T(8,128)(2,1)S(1)} %copy.264) | copy-start | bytes 983044
  22.2 12.9 %copy-start.21 = (f32[128,2,128]{2,1,0:T(2,128)}, f32[128,2,128]{2,1,0:T(2,128)S(1)}, u32[]{:S(2)}) copy-start(f32[128,2,128]{2,1,0:T(2,128)S(1)} %copy.268) | copy-start | bytes 393220
  22.4 24.9 %copy-start.3 = (bf16[1,1,1,128,1280]{3,4,2,1,0:T(8,128)(2,1)}, bf16[1,1,1,128,1280]{3,4,2,1,0:T(8,128)(2,1)S(1)}, u32[]{:S(2)}) copy-start(bf16[1,1,1,128,1280]{3,4,2,1,0:T(8,128)(2,1)S(1)} %copy.261) | copy-start | bytes 983044
  22.8 12.2 %copy-start.22 = (f32[128,2,128]{2,1,0:T(2,128)}, f32[128,2,128]{2,1,0:T(2,128)S(1)}, u32[]{:S(2)}) copy-start(f32[128,2,128]{2,1,0:T(2,128)S(1)} %copy.266) | copy-start | bytes 393220
  22.9 38.2 %copy-start.25 = (pred[128,128]{1,0:T(8,128)(4,1)}, pred[128,128]{1,0:T(8,128)(4,1)S(1)}, u32[]{:S(2)}) copy-start(pred[128,128]{1,0:T(8,128)(4,1)S(1)} %iota_compare_fusion) | copy-start | bytes 49156
  22.9 12.1 %copy-start.23 = (f32[128,2,64]{0,2,1:T(8,128)}, f32[128,2,64]{0,2,1:T(8,128)S(1)}, u32[]{:S(2)}) copy-start(f32[128,2,64]{0,2,1:T(8,128)S(1)} %exponential-minus-one_negate_fusion) | copy-start | bytes 196612
  23.8 13.9 %copy-start.24 = (f32[128,2,64]{0,2,1:T(8,128)}, f32[128,2,64]{0,2,1:T(8,128)S(1)}, u32[]{:S(2)}) copy-start(f32[128,2,64]{0,2,1:T(8,128)S(1)} %exponential-minus-one_negate_fusion.1) | copy-start | bytes 196612
  46.0 11.4 %copy-start.31 = (f32[128]{0:T(128)}, f32[128]{0:T(128)S(1)}, u32[]{:S(2)}) copy-start(f32[128]{0:T(128)S(1)} %fusion.146) | copy-start | bytes 1540
  57.4 143.5 %copy-start.5 = (f32[128,2,1,64]{0,3,1,2:T(8,128)}, f32[128,2,1,64]{0,3,1,2:T(8,128)S(1)}, u32[]{:S(2)}) copy-start(f32[128,2,1,64]{0,3,1,2:T(8,128)S(1)} %copy.207) | copy-start | bytes 196612
  59.0 11.4 %copy-start.29 = (f32[128]{0:T(128)}, f32[128]{0:T(128)S(1)}, u32[]{:S(2)}) copy-start(f32[128]{0:T(128)S(1)} %fusion.147) | copy-start | bytes 1540
  109.1 91.8 %copy-start.6 = (f32[128,2,64]{0,2,1:T(8,128)}, f32[128,2,64]{0,2,1:T(8,128)S(1)}, u32[]{:S(2)}) copy-start(f32[128,2,64]{0,2,1:T(8,128)S(1)} %get-tuple-element.63) | copy-start | bytes 196612
  198.7 2.9 copy-start.7
  200.3 1.3 copy-start.10
  200.9 0.7 copy-start.28
  206.2 0.6 copy-start.11
  206.7 1.6 copy-start.27
  317.7 79.3 %all-reduce.10.cloned.1.call-start = ((), (), s32[]{:S(2)}) async-start(), calls=%async_computation.1 | async-start | bytes 262144 | tf_op jit(solution)/shard_map/psum | solution.py:114
  345.8 36.3 %copy-start.2 = (bf16[1,1,1,128,1280]{3,4,2,1,0:T(8,128)(2,1)S(1)}, bf16[1,1,1,128,1280]{3,4,2,1,0:T(8,128)(2,1)}, u32[]{:S(2)}) copy-start(bf16[1,1,1,128,1280]{3,4,2,1,0:T(8,128)(2,1)} %copy-done.1) | copy-start | bytes 983044
  346.8 0.6 copy-start.14
  349.5 28.5 %copy-start.4 = (bf16[1,1,1,128,1280]{3,4,2,1,0:T(8,128)(2,1)S(1)}, bf16[1,1,1,128,1280]{3,4,2,1,0:T(8,128)(2,1)}, u32[]{:S(2)}) copy-start(bf16[1,1,1,128,1280]{3,4,2,1,0:T(8,128)(2,1)} %copy-done.3) | copy-start | bytes 983044
  349.5 28.5 %copy-start.9 = (f32[128,2,128]{0,2,1:T(8,128)S(1)}, f32[128,2,128]{0,2,1:T(8,128)}, u32[]{:S(2)}) copy-start(f32[128,2,128]{0,2,1:T(8,128)} %copy.222) | copy-start | bytes 393220
  351.1 30.2 %copy-start.15 = (f32[2,64,128]{2,1,0:T(8,128)S(1)}, f32[2,64,128]{2,1,0:T(8,128)}, u32[]{:S(2)}) copy-start(f32[2,64,128]{2,1,0:T(8,128)} %copy-done.14) | copy-start | bytes 196612
  354.8 48.5 %copy-start.26 = (pred[128,128]{1,0:T(8,128)(4,1)S(1)}, pred[128,128]{1,0:T(8,128)(4,1)}, u32[]{:S(2)}) copy-start(pred[128,128]{1,0:T(8,128)(4,1)} %copy-done.25) | copy-start | bytes 49156
  375.3 119.9 %all-reduce.12.cloned.1.call-start = ((), (), s32[]{:S(2)}) async-start(), calls=%async_computation.6 | async-start | bytes 2621440
  377.8 158.0 %all-gather.6.cloned.1.call-start = ((), (), s32[]{:S(2)}) async-start(), calls=%async_computation.2 | async-start | bytes 1392640 | tf_op jit(solution)/shard_map/all_gather | solution.py:116
  403.4 9.3 %copy-start.30 = (f32[128]{0:T(128)S(1)}, f32[128]{0:T(128)}, u32[]{:S(2)}) copy-start(f32[128]{0:T(128)} %copy-done.29) | copy-start | bytes 1540
  403.4 9.7 %copy-start.32 = (f32[8]{0:T(128)S(1)}, f32[8]{0:T(128)}, u32[]{:S(2)}) copy-start(f32[8]{0:T(128)} %psum.15) | copy-start | bytes 100
  403.4 43.3 %copy-start.17 = (f32[128,128]{0,1:T(8,128)S(1)}, f32[128,128]{0,1:T(8,128)}, u32[]{:S(2)}) copy-start(f32[128,128]{0,1:T(8,128)} %get-tuple-element.57) | copy-start | bytes 196612
  403.4 43.7 %copy-start.16 = (f32[128,128]{0,1:T(8,128)S(1)}, f32[128,128]{0,1:T(8,128)}, u32[]{:S(2)}) copy-start(f32[128,128]{0,1:T(8,128)} %get-tuple-element.105) | copy-start | bytes 196612
  403.4 44.1 %copy-start.8 = (bf16[1,1,128,1280]{3,2,0,1:T(8,128)(2,1)S(1)}, bf16[1,1,128,1280]{3,2,0,1:T(8,128)(2,1)}, u32[]{:S(2)}) copy-start(bf16[1,1,128,1280]{3,2,0,1:T(8,128)(2,1)} %copy.182) | copy-start | bytes 983044
Sparse Core Ops, SparseCore 0:
  12.5 90.2 all-gather.9
  105.6 85.7 all-gather.7
  317.8 55.7 reduce-scatter.4
  376.3 20.6 all-reduce.9
  400.9 94.3 all-reduce.11
  497.4 38.3 all-gather.5
